TPU v7x, 32 devices: a whole 2x2x4 slice. The times are simulated.
32 devices in a mesh: leaf: 4 (over y, x), row: 2 (over core), col: 4 (over z).
Axes of the slice: x: 2, y: 2, z: 4, core: 2. Of those that a mesh axis runs over, the one named last changes fastest.
Arguments:
- anc_inverse: float32 [24, 24, 512, 512], P('leaf', None, 'row', 'col'), may hold values from -6 to 6, as said below
- struct_one: int32 [12, 5], P('leaf'), may hold values from 0 to 23, as said below
- lower_one: float32 [12, 5, 512, 512], P('leaf', None, 'row', 'col'), may hold values from -0.125 to 0.125
- pivot_inv_one: float32 [12, 512, 512], P('leaf', 'row', 'col'), may hold values from -6 to 6, as said below
- lower_two: float32 [24, 6, 512, 512], P('leaf', None, 'row', 'col'), may hold values from -0.109375 to 0.109375
- pivot_inv_two: float32 [24, 512, 512], P('leaf', 'row', 'col'), may hold values from -6 to 6, as said below
Outputs:
- offdiag_one: float32 [12, 5, 512, 512], P('leaf', None, 'row', 'col')
- diag_one: float32 [12, 512, 512], P('leaf', 'row', 'col')
- offdiag_two: float32 [24, 6, 512, 512], P('leaf', None, 'row', 'col')
- diag_two: float32 [24, 512, 512], P('leaf', 'row', 'col')
Inputs may be any that keep to these rules, and one draw needn't show every extreme that they name: `struct_one`: each row lists 5 different separator block numbers in increasing order. symmetric: anc_inverse[b, a] is the transpose of anc_inverse[a, b]. `pivot_inv_one`: every block equals its transpose. `pivot_inv_two`: every block equals its transpose.
All inputs are finite; a program needn't handle non-finite values.
Results may differ from a plain program's by a relative error of at most 0.0001.
Values sent between devices are 32-bit elements; how exact they have to be, the bound alone decides.
No kernel may reach another device: no remote copies, remote signals or barrier semaphores. Data moves between devices by JAX's collectives and lax.ppermute only.
A program may use at most 192 MiB of HBM per device.

v0:
```python
import jax
import jax.numpy as jnp
from jax import lax
from jax.sharding import PartitionSpec as P

highest = lax.Precision.HIGHEST


def on_device(anc_inverse, struct_one, lower_one, pivot_inv_one, lower_two, pivot_inv_two):
    level_nodes, struct_len = struct_one.shape
    owned = anc_inverse.shape[0]
    tile_rows = lower_one.shape[2]
    tile_cols = lower_one.shape[3]
    children = lower_two.shape[0] // level_nodes
    one_rows = lax.all_gather(lower_one, "row", axis=2, tiled=True)
    one_cols, two_cols = (
        lax.all_gather(lower_one, "col", axis=3, tiled=True),
        lax.all_gather(lower_two, "col", axis=3, tiled=True),
    )
    all_lists = lax.all_gather(struct_one, "leaf", axis=0, tiled=True)
    first_block = lax.axis_index("leaf") * owned
    local_rows = all_lists - first_block
    inside = ((local_rows >= 0) & (local_rows < owned)).astype(jnp.float32)
    clipped = jnp.clip(local_rows, 0, owned - 1)
    columns = anc_inverse[:, all_lists]
    node_index = jnp.arange(all_lists.shape[0], dtype=jnp.int32)[:, None]
    partial_value = columns[clipped, node_index] * inside[:, :, None, None, None]
    selected = lax.psum_scatter(partial_value, "leaf", scatter_dimension=0, tiled=True)
    stripes = lax.all_gather(selected, "col", axis=4, tiled=True)
    offdiag_one = -jnp.einsum("mstik,mtkj->msij", stripes, one_rows, precision=highest)
    cols_piece = one_cols
    summed_one = lax.psum_scatter(
        jnp.einsum("mski,mskj->imj", cols_piece, offdiag_one, precision=highest),
        "row",
        scatter_dimension=0,
        tiled=True,
    )
    diag_one = pivot_inv_one - jnp.transpose(summed_one, (1, 0, 2))
    parent_col = jnp.concatenate([offdiag_one, diag_one[:, None]], axis=1)
    parent_stripe = lax.all_gather(parent_col, "col", axis=3, tiled=True)
    two_rows = lax.all_gather(lower_two, "row", axis=2, tiled=True)
    rows_split = two_rows.reshape(
        level_nodes, children, struct_len + 1, two_rows.shape[2], tile_cols
    )
    cols_split = two_cols.reshape(
        level_nodes, children, struct_len + 1, tile_rows, two_cols.shape[3]
    )
    local_split = lower_two.reshape(level_nodes, children, struct_len + 1, tile_rows, tile_cols)
    upper_part = jnp.einsum(
        "mstik,mctkj->mcsij", stripes, rows_split[:, :, :struct_len], precision=highest
    )
    upper_part = upper_part + jnp.einsum(
        "msik,mckj->mcsij",
        parent_stripe[:, :struct_len],
        rows_split[:, :, struct_len],
        precision=highest,
    )
    stripe_piece = parent_stripe[:, :struct_len]
    summed_parent = lax.psum_scatter(
        jnp.einsum(
            "mqki,mcqkj->imcj", stripe_piece, local_split[:, :, :struct_len], precision=highest
        ),
        "row",
        scatter_dimension=0,
        tiled=True,
    )
    parent_row = jnp.transpose(summed_parent, (1, 2, 0, 3))
    parent_row = parent_row + jnp.einsum(
        "mik,mckj->mcij",
        parent_stripe[:, struct_len],
        rows_split[:, :, struct_len],
        precision=highest,
    )
    offdiag_split = -jnp.concatenate([upper_part, parent_row[:, :, None]], axis=2)
    cols_piece = cols_split
    summed_two = lax.psum_scatter(
        jnp.einsum("mcpki,mcpkj->imcj", cols_piece, offdiag_split, precision=highest),
        "row",
        scatter_dimension=0,
        tiled=True,
    )
    diag_two = pivot_inv_two - jnp.transpose(summed_two, (1, 2, 0, 3)).reshape(
        level_nodes * children, tile_rows, tile_cols
    )
    offdiag_two = offdiag_split.reshape(
        level_nodes * children, struct_len + 1, tile_rows, tile_cols
    )
    return (offdiag_one, diag_one, offdiag_two, diag_two)


def solution(mesh):
    placed = (
        P("leaf", None, "row", "col"),
        P("leaf", None),
        P("leaf", None, "row", "col"),
        P("leaf", "row", "col"),
        P("leaf", None, "row", "col"),
        P("leaf", "row", "col"),
    )
    return jax.shard_map(
        on_device,
        mesh=mesh,
        in_specs=placed,
        out_specs=(
            P("leaf", None, "row", "col"),
            P("leaf", "row", "col"),
            P("leaf", None, "row", "col"),
            P("leaf", "row", "col"),
        ),
        check_vma=False,
    )
```

profile of v0, /device:TPU:0, one launch (start us, length us, event | category | flops | bytes accessed | tf_op | source)
XLA Modules:
  0.0 1826.3 jit_solution(5516012726948802101)
XLA Ops:
  8.0 0.0 reduce-scatter.13.cloned.1.call-start
  8.0 9.7 all-gather
  17.8 0.1 copy.56
  17.9 0.1 copy.33
  18.0 0.1 reshape.39
  18.1 0.1 copy.32
  18.2 0.1 reshape.33
  18.3 0.1 copy.34
  18.4 34.3 %gather_fusion = f32[60,6,256,128]{3,2,1,0:T(8,128)} fusion(f32[6,24,256,128]{3,2,1,0:T(8,128)} %param.6, s32[1024]{0:T(1024)S(1)} %pad_clamp_fusion), kind=kCustom, calls=%fused_computation | custom fusion | bytes 94372080 | tf_op jit(solution)/shard_map/gather | solution.py:25
  52.7 28.4 %gather_fusion.1 = f32[60,5,256,128]{3,2,1,0:T(8,128)} fusion(f32[6,12,5,256,128]{4,3,0,2,1:T(8,128)} %bitcast.113, s32[60]{0:T(128)S(1)} %reshape.39), kind=kCustom, calls=%fused_computation.1 | custom fusion | bytes 78643680 | tf_op jit(solution)/shard_map/gather | solution.py:27
  81.1 28.0 %broadcast_multiply_fusion = f32[12,5,5,256,128]{4,3,2,1,0:T(8,128)} fusion(f32[12,5,5,256,128]{4,3,2,1,0:T(8,128)} %bitcast.114, f32[12,5]{1,0:T(8,128)S(1)} %copy.34), kind=kLoop, calls=%fused_computation.4 | loop fusion | flops 9830400 | bytes 78643440 | tf_op jit(solution)/shard_map/mul | solution.py:27
  109.0 0.0 reduce-scatter.13.cloned.1.call-update
  109.1 0.0 all-gather.10.cloned.1.call-start
  109.1 0.5 all-gather.10.cloned.1.call-update
  109.6 0.0 all-gather.8.cloned.1.call-start
  109.7 334.9 %reduce-scatter.13.cloned.1.call-done = f32[3,5,5,256,128]{4,3,2,1,0:T(8,128)} async-done(((f32[12,5,5,256,128]{4,3,2,1,0:T(8,128)}), f32[3,5,5,256,128]{4,3,2,1,0:T(8,128)}) %reduce-scatter.13.cloned.1.call-update) | async-done | bytes 9830416
  444.6 0.0 all-gather.8.cloned.1.call-update
  444.6 0.0 all-gather.12.cloned.1.call-start
  444.6 0.5 all-gather.12.cloned.1.call-update
  445.2 0.6 reduce-scatter.7.cloned.1.call-start
  445.7 0.0 all-gather.10.cloned.1.call-done
  445.8 655.6 %all-gather.8.cloned.1.call-done = f32[3,5,5,256,512]{4,3,2,1,0:T(8,128)} async-done(((f32[3,5,5,256,128]{4,3,2,1,0:T(8,128)}), f32[3,5,5,256,512]{4,3,2,1,0:T(8,128)}) %all-gather.8.cloned.1.call-update) | async-done | bytes 39321616 | tf_op jit(solution)/shard_map/all_gather | solution.py:29
  1101.4 37.0 %bitcast_negate_fusion = f32[3,5,256,128]{3,2,1,0:T(8,128)S(1)} fusion(f32[3,5,5,256,512]{4,3,2,1,0:T(8,128)} %all-gather.8.cloned.1.call-done, f32[3,5,512,128]{3,2,1,0:T(8,128)} %all-gather.10.cloned.1.call-done), kind=kOutput, calls=%fused_computation.22 | convolution fusion | flops 15099985920 | bytes 45219840 | tf_op jit(solution)/shard_map/mstik,mtkj->msij/dot_general | solution.py:30
  1138.4 0.0 copy-start
  1138.4 0.0 copy-start.3
  1138.4 103.0 %all-gather.12.cloned.1.call-done = f32[3,5,256,512]{3,2,1,0:T(8,128)} async-done(((f32[3,5,256,128]{3,2,1,0:T(8,128)}), f32[3,5,256,512]{3,2,1,0:T(8,128)}) %all-gather.12.cloned.1.call-update) | async-done | bytes 7864336 | tf_op jit(solution)/shard_map/all_gather | solution.py:17
  1241.4 15.4 convolution_bitcast_fusion
  1256.8 0.0 reduce-scatter.7.cloned.1.call-update
  1256.8 0.0 all-gather.16.cloned.1.call-start
  1256.9 6.3 reduce-scatter.7.cloned.1.call-done
  1263.2 0.0 copy-done.3
  1263.2 1.0 bitcast_subtract_fusion
  1264.3 0.0 copy-start.1
  1264.3 0.0 copy-done
  1264.3 1.6 pad_maximum_fusion
  1265.9 0.0 all-gather.16.cloned.1.call-update
  1265.9 0.0 all-gather.14.cloned.1.call-start
  1265.9 0.7 all-gather.14.cloned.1.call-update
  1266.6 0.0 copy-done.1
  1266.6 0.2 reduce-scatter.9.cloned.1.call-start
  1266.8 166.4 %all-gather.16.cloned.1.call-done = f32[3,6,256,512]{3,2,1,0:T(8,128)} async-done(((f32[3,6,256,128]{3,2,1,0:T(8,128)}), f32[3,6,256,512]{3,2,1,0:T(8,128)}) %all-gather.16.cloned.1.call-update) | async-done | bytes 9437200 | tf_op jit(solution)/shard_map/all_gather | solution.py:40
  1433.2 17.2 fusion.24
  1450.4 0.0 reduce-scatter.9.cloned.1.call-update
  1450.4 0.0 all-gather.18.cloned.1.call-start
  1450.5 0.5 all-gather.18.cloned.1.call-update
  1451.0 0.3 reduce-scatter.11.cloned.1.call-start
  1451.3 3.2 all-gather.14.cloned.1.call-done
  1454.5 35.3 %fusion = f32[3,5,256,2,128,1]{4,2,5,3,1,0:T(8,128)S(1)} fusion(f32[3,5,5,256,512]{4,3,2,1,0:T(8,128)} %all-gather.8.cloned.1.call-done, f32[3,2,6,512,128]{4,3,2,1,0:T(8,128)} %bitcast.118), kind=kOutput, calls=%fused_computation.2 | convolution fusion | flops 30198988800 | bytes 51118080 | tf_op jit(solution)/shard_map/mstik,mctkj->mcsij/dot_general | solution.py:49
  1489.8 11.3 fusion.13
  1501.1 0.0 reduce-scatter.9.cloned.1.call-done
  1501.1 3.8 fusion.34
  1504.9 287.1 %all-gather.18.cloned.1.call-done = f32[6,6,256,512]{3,2,1,0:T(8,128)} async-done(((f32[6,6,256,128]{3,2,1,0:T(8,128)}), f32[6,6,256,512]{3,2,1,0:T(8,128)}) %all-gather.18.cloned.1.call-update) | async-done | bytes 18874384 | tf_op jit(solution)/shard_map/all_gather | solution.py:18
  1792.1 16.8 fusion.21
  1808.9 0.0 reduce-scatter.11.cloned.1.call-update
  1808.9 2.5 copy.37
  1811.4 0.0 copy-start.2
  1811.5 2.8 maximum_negate_fusion
  1814.2 1.8 reduce-scatter.11.cloned.1.call-done
  1816.0 1.4 copy.41
  1817.4 0.0 copy-done.2
  1817.4 1.0 sub.15
  (5 shorter events, 0.0 us)
Async XLA Ops:
  8.0 436.6 %reduce-scatter.13.cloned.1.call-start = ((), (), s32[]{:S(2)}) async-start(), calls=%async_computation.13 | async-start | bytes 49152000
  109.1 336.7 %all-gather.10.cloned.1.call-start = ((), (), s32[]{:S(2)}) async-start(), calls=%async_computation.5 | async-start | bytes 5898240 | tf_op jit(solution)/shard_map/all_gather | solution.py:15
  109.6 991.7 %all-gather.8.cloned.1.call-start = ((), (), s32[]{:S(2)}) async-start(), calls=%async_computation.4 | async-start | bytes 49152000 | tf_op jit(solution)/shard_map/all_gather | solution.py:29
  444.6 796.8 %all-gather.12.cloned.1.call-start = ((), (), s32[]{:S(2)}) async-start(), calls=%async_computation.6 | async-start | bytes 9830400 | tf_op jit(solution)/shard_map/all_gather | solution.py:17
  445.2 818.1 %reduce-scatter.7.cloned.1.call-start = ((), (), s32[]{:S(2)}) async-start(), calls=%async_computation.7 | async-start | bytes 1179648 | tf_op jit(solution)/shard_map/reduce_scatter | solution.py:32
  1138.4 125.9 %copy-start = (f32[3,5,256,128]{3,2,1,0:T(8,128)}, f32[3,5,256,128]{3,2,1,0:T(8,128)S(1)}, u32[]{:S(2)}) copy-start(f32[3,5,256,128]{3,2,1,0:T(8,128)S(1)} %bitcast_negate_fusion) | copy-start | bytes 5898244
  1138.4 124.8 %copy-start.3 = (f32[3,256,128]{2,1,0:T(8,128)S(1)}, f32[3,256,128]{2,1,0:T(8,128)}, u32[]{:S(2)}) copy-start(f32[3,256,128]{2,1,0:T(8,128)} %param.9) | copy-start | bytes 1179652
  1256.8 176.4 %all-gather.16.cloned.1.call-start = ((), (), s32[]{:S(2)}) async-start(), calls=%async_computation.9 | async-start | bytes 11796480 | tf_op jit(solution)/shard_map/all_gather | solution.py:40
  1264.3 2.4 copy-start.1
  1265.9 188.6 %all-gather.14.cloned.1.call-start = ((), (), s32[]{:S(2)}) async-start(), calls=%async_computation.8 | async-start | bytes 14155776 | tf_op jit(solution)/shard_map/all_gather | solution.py:41
  1266.6 234.5 %reduce-scatter.9.cloned.1.call-start = ((), (), s32[]{:S(2)}) async-start(), calls=%async_computation.10 | async-start | bytes 2359296 | tf_op jit(solution)/shard_map/reduce_scatter | solution.py:59
  1450.4 341.6 %all-gather.18.cloned.1.call-start = ((), (), s32[]{:S(2)}) async-start(), calls=%async_computation.11 | async-start | bytes 23592960 | tf_op jit(solution)/shard_map/all_gather | solution.py:18
  1451.0 365.0 %reduce-scatter.11.cloned.1.call-start = ((), (), s32[]{:S(2)}) async-start(), calls=%async_computation.12 | async-start | bytes 2359296 | tf_op jit(solution)/shard_map/reduce_scatter | solution.py:76
  1811.4 6.0 copy-start.2
Sparse Core Ops, SparseCore 0:
  109.2 335.3 reduce-scatter.12
Sparse Core Ops, SparseCore 1:
  111.1 13.4 all-gather.9
  444.7 656.6 all-gather.7
  1102.8 138.6 all-gather.11
  1256.9 6.3 reduce-scatter.6
  1266.0 167.2 all-gather.15
  1434.8 19.7 all-gather.13
  1456.6 10.0 reduce-scatter.8
  1468.1 323.9 all-gather.17
  1809.0 7.0 reduce-scatter.10
where the time goes:
time: 1830 us
  waiting for transfers between devices  1560 us (85%)
  matrix products  137 us (7%)
  local copies, waits for them, and re-layouts  67.2 us (4%)
  other arithmetic  34.3 us (2%)
    all_gather x1, waiting for transfers between devices, on_device(): stripes = lax.all_gather(selected, 'col', axis=4, tiled=True)  656 us
    unnamed x11, waiting for transfers between devices  337 us
    all_gather x1, waiting for transfers between devices, on_device(): lax.all_gather(lower_two, 'col', axis=3, tiled=True)  287 us
    all_gather x1, waiting for transfers between devices, on_device(): parent_stripe = lax.all_gather(parent_col, 'col', axis=3, tiled=True)  166 us
    all_gather x1, waiting for transfers between devices, on_device(): lax.all_gather(lower_one, 'col', axis=3, tiled=True)  103 us
    dot_general x1, matrix products, on_device(): jnp.einsum('mstik,mtkj->msij', stripes, one_rows, precision=highest)  37 us
  transfers between devices with their start and end apart: 10, of which 8 were waited for; matrix products, arithmetic and copies ran while one was open for 6% of the time, Pallas kernels for 0%

commit v1 on v0

v1 whole, which is shorter than its diff:
```python
import jax
import jax.numpy as jnp
from jax import lax
from jax.experimental import pallas as pl
from jax.experimental.pallas import tpu as pltpu
from jax.sharding import PartitionSpec as P


def select(anc, rows, cols):
    owned, blocks, tr, tc = anc.shape
    dests, pairs = rows.shape
    group = max(n for n in range(1, 6) if pairs % n == 0)
    have = (rows >= 0) & (rows < owned)
    index = jnp.where(have, rows * blocks + cols, 0).reshape(-1)
    flat = anc.reshape(owned * blocks, tr, tc)

    def kernel(index_ref, have_ref, *refs):
        out = refs[group]
        for j in range(group):
            keep = have_ref[pl.program_id(0) * group + j]

            @pl.when(keep == 1)
            def _():
                out[j] = refs[j][0]

            @pl.when(keep == 0)
            def _():
                out[j] = jnp.zeros((tr, tc), jnp.float32)

    def block(j):
        return pl.BlockSpec((1, tr, tc), lambda g, i, h: (i[g * group + j], 0, 0))

    return pl.pallas_call(
        kernel,
        grid_spec=pltpu.PrefetchScalarGridSpec(
            num_scalar_prefetch=2,
            grid=(dests * pairs // group,),
            in_specs=[block(j) for j in range(group)],
            out_specs=pl.BlockSpec((group, tr, tc), lambda g, i, h: (g, 0, 0)),
        ),
        out_shape=jax.ShapeDtypeStruct((dests * pairs, tr, tc), anc.dtype),
        name="select_blocks",
    )(index, have.astype(jnp.int32).reshape(-1), *[flat] * group).reshape(dests, pairs, tr, tc)


def split(value):
    top = value.astype(jnp.bfloat16)
    return top, (value - top.astype(jnp.float32)).astype(jnp.bfloat16)


def split_dot(left, right, dims):
    def product(x, y):
        return lax.dot_general(x, y, (dims, ((), ())), preferred_element_type=jnp.float32)

    (left_top, left_low), (right_top, right_low) = left, right
    return product(left_top, right_top) + (
        product(left_top, right_low) + product(left_low, right_top)
    )


def by_position(where, pieces, out, sems, size):
    tc = pieces[0].shape[2]
    for at in range(size):
        for here in range(size):

            @pl.when(where == here)
            def _():
                pltpu.make_async_copy(
                    pieces[size - 1 + at - here],
                    out.at[:, :, pl.ds(at * tc, tc)],
                    sems.at[at],
                ).start()


def wait_positions(pieces, out, sems, size):
    tc = pieces[0].shape[2]
    for at in range(size):
        pltpu.make_async_copy(
            pieces[size - 1], out.at[:, :, pl.ds(at * tc, tc)], sems.at[at]
        ).wait()


anywhere = pl.BlockSpec(memory_space=pl.ANY)
scalars = pl.BlockSpec(memory_space=pltpu.SMEM)
local = pl.BlockSpec(memory_space=pltpu.VMEM)
row_row = ((0,), (0,))
plain = ((1,), (0,))


def change_base(parts, two, t_rows, place, size):
    count, tr, tc = parts[0].shape
    length = count - 1
    children = two.shape[0]
    many = len(parts)

    def kernel(where, *refs):
        pieces = refs[:many]
        two_ref, t_ref, right, pivot, full, held, sems = refs[many:]
        by_position(where[0], pieces, held, sems, size)
        terms = [split(t_ref[k]) for k in range(children)]
        wait_positions(pieces, held, sems, size)

        for k in range(children):
            pivot[k] = split_dot(split(held[length]), terms[k], plain)

        for s in range(length):
            whole = held[s]
            full[s] = whole
            both = split(whole)
            for k in range(children):
                changed = two_ref[k, s] - split_dot(both, terms[k], plain)
                right[s, :, pl.ds((k + 1) * tc, tc)] = changed
        for here in range(size):

            @pl.when(where[0] == here)
            def _():
                right[:, :, pl.ds(0, tc)] = held[pl.ds(0, length), :, pl.ds(here * tc, tc)]

    shape = lambda *dims: jax.ShapeDtypeStruct(dims, jnp.float32)
    return pl.pallas_call(
        kernel,
        in_specs=[scalars] + [anywhere] * many + [local, local],
        out_specs=(local, local, local),
        out_shape=(
            shape(length, tr, (children + 1) * tc),
            shape(children, tr, tc),
            shape(length, tr, size * tc),
        ),
        scratch_shapes=[
            pltpu.VMEM((count, tr, size * tc), jnp.float32),
            pltpu.SemaphoreType.DMA((size,)),
        ],
        name="change_base",
    )(place.reshape(1), *parts, two, t_rows)


def share(whole, keep, sends, row_at, tr, axis):
    for step, out in enumerate([keep, *sends]):
        owner = lax.rem(row_at + step, len(sends) + 1)
        rows = pl.ds(pl.multiple_of(owner * tr, tr), tr)
        out[...] = whole[rows] if axis == 0 else whole[:, rows]


def multiply(parts, rights, place, row_place, table, size):
    count, tr, tc = parts[0].shape
    length, _, wide = rights[0].shape
    width = size * tc
    many, shares = len(parts), len(rights)

    def kernel(where, row_at, pair, *refs):
        pieces, given = refs[:many], refs[many : many + shares]
        direct, top, low, *outs = refs[many + shares : -3]
        held, turned, sems = refs[-3:]
        by_position(where[0], pieces, held, sems, size)
        for step, right in enumerate(given):
            owner = lax.rem(row_at[0] + shares - step, shares)
            rows = pl.ds(pl.multiple_of(owner * tr, tr), tr)
            for p in range(length):
                top[p, rows], low[p, rows] = split(right[p])
        direct[...] = jnp.zeros_like(direct)
        turned[...] = jnp.zeros_like(turned)
        start = pl.multiple_of(row_at[0] * tr, tr)
        wait_positions(pieces, held, sems, size)

        def step(t, carry):
            p, q = pair[0, t], pair[1, t]
            block = split(held[t])
            direct[p] += split_dot(block, (top[q], low[q]), plain)
            mine = (top[p, pl.ds(start, tr)], low[p, pl.ds(start, tr)])
            turned[q - 1] += split_dot(block, mine, row_row)
            return carry

        lax.fori_loop(0, count, step, 0)
        share(turned, outs[0], outs[1:], row_at[0], tr, 1)

    return pl.pallas_call(
        kernel,
        in_specs=[scalars] * 3 + [anywhere] * many + [local] * shares,
        out_specs=(local,) * (3 + shares),
        out_shape=(
            jax.ShapeDtypeStruct((length, tr, wide), jnp.float32),
            jax.ShapeDtypeStruct((length, width, wide), jnp.bfloat16),
            jax.ShapeDtypeStruct((length, width, wide), jnp.bfloat16),
            *[jax.ShapeDtypeStruct((length - 1, tr, wide), jnp.float32)] * shares,
        ),
        scratch_shapes=[
            pltpu.VMEM((count, tr, width), jnp.float32),
            pltpu.VMEM((length - 1, width, wide), jnp.float32),
            pltpu.SemaphoreType.DMA((size,)),
        ],
        name="multiply",
    )(place.reshape(1), row_place.reshape(1), table, *parts, *rights)


def finish(parts, top, low, direct, turned, one_full, place, row_place, size, before, m, nodes):
    length, tr, wide = direct.shape
    width = top.shape[1]
    tc = parts[0].shape[2]
    many, shares = len(parts), len(turned)
    chained = [] if before is None else [before]
    fixed = many + 4 + shares

    def kernel(where, row_at, *refs):
        pieces = refs[:many]
        top_ref, low_ref, direct_ref, one_ref = refs[many : many + 4]
        sums = refs[many + 4 : fixed]
        product, off, *outs = refs[fixed + len(chained) : -5]
        held, staged, below, sems, sem = refs[-5:]
        by_position(where[0], pieces, held, sems, size)
        below[...] = jnp.zeros_like(below)
        product[0] = direct_ref[0]
        for p in range(1, length):
            value = direct_ref[p]
            for turned_ref in sums:
                value = value + turned_ref[p - 1]
            product[p] = value
        wait_positions(pieces, held, sems, size)

        def step(p, carry):
            value = product[p] + split_dot(split(held[p]), (top_ref[p], low_ref[p]), plain)
            product[p] = value
            staged[p] = -value[:, :tc]
            below[...] += split_dot(split(one_ref[p]), split(value), row_row)
            return carry

        lax.fori_loop(0, length, step, 0)
        out = pltpu.make_async_copy(staged, off.at[m], sem)
        out.start()
        share(below, outs[0], outs[1:], row_at[0], tr, 0)
        out.wait()

    shape = lambda *dims: jax.ShapeDtypeStruct(dims, jnp.float32)
    return pl.pallas_call(
        kernel,
        in_specs=[scalars] * 2
        + [anywhere] * many
        + [local] * (4 + shares)
        + [anywhere] * len(chained),
        out_specs=(local, anywhere) + (local,) * shares,
        out_shape=(
            shape(length, tr, wide),
            shape(nodes, length, tr, tc),
            *[shape(tr, wide)] * shares,
        ),
        scratch_shapes=[
            pltpu.VMEM((length, tr, width), jnp.float32),
            pltpu.VMEM((length, tr, tc), jnp.float32),
            pltpu.VMEM((width, wide), jnp.float32),
            pltpu.SemaphoreType.DMA((size,)),
            pltpu.SemaphoreType.DMA,
        ],
        input_output_aliases={2 + fixed: 1} if chained else {},
        name="finish",
    )(
        place.reshape(1), row_place.reshape(1), *parts, top, low, direct, one_full, *turned,
        *chained,
    )


def symmetric_upper(product, pieces, holders, place):
    length, tr, _ = product.shape
    keys = sorted(pieces)
    tc = pieces[keys[0]].shape[2]

    def kernel(where, product_ref, *refs):
        given, out = dict(zip(keys, refs)), refs[-1]
        for k in sorted({j for j, _ in keys}):
            column = product_ref[:, :, pl.ds((k + 1) * tc, tc)]
            column = split(column.reshape(length * tr, tc))
            for index, key in enumerate(keys):
                if key[0] != k:
                    continue
                used = where[0] == holders[key][0]
                for here in holders[key][1:]:
                    used = used | (where[0] == here)

                @pl.when(used)
                def _():
                    piece = split(given[key][...].reshape(length * tr, tc))
                    out[index] = split_dot(piece, column, row_row)

    block = pl.BlockSpec((length, tr, tc), lambda i: (0, 0, 0))
    return pl.pallas_call(
        kernel,
        grid=(1,),
        in_specs=[scalars, pl.BlockSpec(product.shape, lambda i: (0, 0, 0))]
        + [block] * len(keys),
        out_specs=pl.BlockSpec((len(keys), tc, tc), lambda i: (0, 0, 0)),
        out_shape=jax.ShapeDtypeStruct((len(keys), tc, tc), jnp.float32),
        name="symmetric_upper",
    )(place.reshape(1), product, *[pieces[key] for key in keys])


def symmetric_last(
    product, below, pivot, own_pivot, upper, pieces, holders, place, size, before, m, nodes
):
    length, tr, wide = product.shape
    children = pivot.shape[0]
    tc = pivot.shape[2]
    keys = sorted(pieces)
    chained = [] if before is None else [before]
    shares = len(below)

    def kernel(where, product_ref, pivot_ref, own_ref, upper_ref, *refs):
        parts, given = refs[:shares], dict(zip(keys, refs[shares:]))
        diag, base, off, out, staged, total, sem = refs[shares + len(keys) + len(chained) :]
        value = parts[0][...]
        for part in parts[1:]:
            value = value + part[...]
        total[...] = value
        for k in range(children):
            span = pl.ds((k + 1) * tc, tc)
            staged[k, pl.ds(0, length)] = -product_ref[:, :, span]
            staged[k, length] = total[:, span] - pivot_ref[k]
        copy = pltpu.make_async_copy(staged, off.at[m], sem)
        copy.start()
        diag[...] = own_ref[...] + total[:, pl.ds(0, tc)]
        base[...] = jnp.zeros_like(base)
        out[...] = jnp.zeros_like(out)
        for k in range(children):
            column = split(pivot_ref[k] - total[:, pl.ds((k + 1) * tc, tc)])
            for index, (j, away) in enumerate(keys):
                if j != k:
                    continue
                for here in holders[k, away]:

                    @pl.when(where[0] == here)
                    def _():
                        piece = split(given[k, away][0])
                        tile = upper_ref[index] + split_dot(piece, column, row_row)
                        base[here + away, k] = tile
                        if away != 0:
                            out[away % size - 1, k] = tile.T

        copy.wait()

    shape = lambda *dims: jax.ShapeDtypeStruct(dims, jnp.float32)
    whole = lambda value: pl.BlockSpec(value.shape, lambda i: (0,) * len(value.shape))
    block = pl.BlockSpec((1, tr, tc), lambda i: (length, 0, 0))
    shapes = [
        shape(tr, tc),
        shape(size, children, tc, tc),
        shape(nodes, children, length + 1, tr, tc),
        shape(size - 1, children, tc, tc),
    ]
    inputs = [product, pivot, own_pivot, upper, *below]
    diag, base, off, out = pl.pallas_call(
        kernel,
        grid=(1,),
        in_specs=[scalars, *map(whole, inputs), *[block] * len(keys), *[anywhere] * len(chained)],
        out_specs=tuple(anywhere if i == 2 else whole(o) for i, o in enumerate(shapes)),
        out_shape=tuple(shapes),
        scratch_shapes=[
            pltpu.VMEM((children, length + 1, tr, tc), jnp.float32),
            pltpu.VMEM((tr, wide), jnp.float32),
            pltpu.SemaphoreType.DMA,
        ],
        input_output_aliases={1 + len(inputs) + len(keys): 2} if chained else {},
        name="symmetric_last",
    )(place.reshape(1), *inputs, *[pieces[key] for key in keys], *chained)
    return off, diag, base, out


def put_back(base, got, place, row_place, tr, shares):
    size, children, tc, _ = base.shape

    def kernel(where, row_at, base_ref, *refs):
        given, outs, whole = refs[: size - 1], refs[size - 1 : -1], refs[-1]
        for k in range(children):
            for at in range(size):
                whole[k, pl.ds(at * tc, tc)] = base_ref[at, k]
            for step in range(1, size):
                source = lax.rem(where[0] + size - step, size)
                rows = pl.ds(pl.multiple_of(source * tc, tc), tc)
                whole[k, rows] += given[step - 1][k]
        share(whole, outs[0], outs[1:], row_at[0], tr, 1)

    return pl.pallas_call(
        kernel,
        in_specs=[scalars] * 2 + [local] * size,
        out_specs=(local,) * shares,
        out_shape=(jax.ShapeDtypeStruct((children, tr, tc), jnp.float32),) * shares,
        scratch_shapes=[pltpu.VMEM((children, size * tc, tc), jnp.float32)],
        name="put_back",
    )(place.reshape(1), row_place.reshape(1), base, *got)


def along_row(value, step):
    count = lax.axis_size("row")
    return lax.ppermute(value, "row", [(i, (i + step) % count) for i in range(count)])


def spread(keep, sends):
    return [keep] + [along_row(value, step + 1) for step, value in enumerate(sends)]


def hop(value, pairs):
    return lax.ppermute(value, "col", pairs)


def line_gather(value, size):
    rights, lefts = [value], [value]
    for step in range(1, size):
        rights.append(hop(rights[-1], [(i, i + 1) for i in range(step - 1, size - 1)]))
        lefts.append(hop(lefts[-1], [(i + 1, i) for i in range(size - step)]))
    return rights[:0:-1] + lefts


def computes(low, high_at, child, size):
    off_low, off_high = abs(2 * low - size + 1), abs(2 * high_at - size + 1)
    if off_low == off_high:
        return high_at if child % 2 == 0 else low
    return low if off_low < off_high else high_at


def pair_gather(value, child, size):
    pieces, holders = {0: value}, {0: list(range(size))}
    for sign in (1, -1):
        moving = value
        for step in range(1, size):
            pairs, uses = [], []
            for source in range(size):
                ends = [
                    end
                    for end in range(size)
                    if (end - source) * sign >= step
                    and computes(min(source, end), max(source, end), child, size) == end
                ]
                if ends:
                    pairs.append((source + sign * (step - 1), source + sign * step))
                    if source + sign * step in ends:
                        uses.append(source + sign * step)
            if not pairs:
                break
            moving = hop(moving, pairs)
            if uses:
                pieces[-sign * step], holders[-sign * step] = moving, uses
    return pieces, holders


def on_device(anc_inverse, struct_one, lower_one, pivot_inv_one, lower_two, pivot_inv_two):
    nodes, length = struct_one.shape
    owned = anc_inverse.shape[0]
    tr, tc = lower_one.shape[2:]
    children = lower_two.shape[0] // nodes
    size, place = lax.axis_size("col"), lax.axis_index("col")
    row_place = lax.axis_index("row")
    two = lower_two.reshape(nodes, children, length + 1, tr, tc)
    apart = [(p, q) for p in range(length) for q in range(p + 1, length)]
    pairs = apart + [(p, p) for p in range(length)]
    first = jnp.array([p for p, _ in pairs], jnp.int32)
    second = jnp.array([q for _, q in pairs], jnp.int32)
    table = jnp.stack([first, second])

    pieces_one = [
        line_gather(jnp.concatenate([lower_one[m], pivot_inv_one[m][None]]), size)
        for m in range(nodes)
    ]
    lists = lax.all_gather(struct_one, "leaf", axis=0, tiled=False)
    near = lists - lax.axis_index("leaf") * owned
    t_rows = lax.all_gather(two[:, :, length], "row", axis=2, tiled=True)
    picked = []
    for m in range(nodes):
        parts = []
        for span in (slice(0, len(apart)), slice(len(apart), len(pairs))):
            mine = select(
                anc_inverse, near[:, m][:, first[span]], lists[:, m][:, second[span]]
            )
            parts.append(lax.psum_scatter(mine, "leaf", scatter_dimension=0, tiled=False))
        picked.append(parts)
    given, holders = [], {}
    for m in range(nodes):
        pieces = {}
        for k in range(children):
            found, uses = pair_gather(two[m, k], k, size)
            for away, piece in found.items():
                pieces[k, away], holders[k, away] = piece, uses[away]
        given.append(pieces)
    bases = []
    for m in range(nodes):
        bases.append(change_base(pieces_one[m], two[m], t_rows[m], place, size))
    off_one, off_two = None, None
    diags_one, diags_two = [], []
    shares = lax.axis_size("row")
    for m in range(nodes):
        right, pivot, one_full = bases[m]
        rights = spread(right, [right] * (shares - 1))
        apart_parts = line_gather(picked[m][0], size)
        same_parts = line_gather(picked[m][1], size)
        direct, top, low, *turned = multiply(
            apart_parts, rights, place, row_place, table, size
        )
        turned = spread(turned[0], turned[1:])
        product, off_one, *below = finish(
            same_parts, top, low, direct, turned, one_full, place, row_place, size,
            off_one, m, nodes,
        )
        below = spread(below[0], below[1:])
        upper = symmetric_upper(product, given[m], holders, place)
        off_two, diag_one, base, sends = symmetric_last(
            product, below, pivot, pivot_inv_one[m], upper, given[m], holders,
            place, size, off_two, m, nodes,
        )
        got = []
        for step in range(1, size):
            moves = [
                (here, (here + away) % size)
                for (_, away), uses in holders.items()
                for here in uses
                if away != 0 and away % size == step
            ]
            got.append(hop(sends[step - 1], sorted(set(moves))))
        keep, *sends = put_back(base, got, place, row_place, tr, shares)
        summed = spread(keep, sends)
        diags_one.append(diag_one)
        diags_two.append(pivot_inv_two.reshape(nodes, children, tr, tc)[m] + sum(summed[1:], summed[0]))
    return (
        off_one,
        jnp.stack(diags_one),
        off_two.reshape(lower_two.shape),
        jnp.stack(diags_two).reshape(pivot_inv_two.shape),
    )


def solution(mesh):
    placed = (
        P("leaf", None, "row", "col"),
        P("leaf", None),
        P("leaf", None, "row", "col"),
        P("leaf", "row", "col"),
        P("leaf", None, "row", "col"),
        P("leaf", "row", "col"),
    )
    return jax.shard_map(
        on_device,
        mesh=mesh,
        in_specs=placed,
        out_specs=(
            P("leaf", None, "row", "col"),
            P("leaf", "row", "col"),
            P("leaf", None, "row", "col"),
            P("leaf", "row", "col"),
        ),
        check_vma=False,
    )
```

time: 1830 us -> 975 us (0.53)
  waiting for transfers between devices: 1560 us -> 478 us
  starting transfers between devices: 1.33 us -> 214 us
  Pallas kernels: 0 us -> 199 us
  matrix products: 137 us -> 0 us
  other arithmetic: 34.3 us -> 5.18 us
  local copies, waits for them, and re-layouts: 67.2 us -> 42 us
    all_gather x6 -> x1, waiting for transfers between devices: 1220 us -> 0.02 us  [on_device(): t_rows = lax.all_gather(two[:, :, length], 'row', axis=2, tiled=True)]
    ppermute x0 -> x105, waiting for transfers between devices: none -> 477 us  [the longest x93 476 us: hop(): return lax.ppermute(value, 'col', pairs)]
    unnamed x11 -> x13, waiting for transfers between devices: 337 us -> 0.23 us
    ppermute x0 -> x105, starting transfers between devices: none -> 213 us  [the longest x93 211 us: hop(): return lax.ppermute(value, 'col', pairs)]
    pallas_call x0 -> x24, Pallas kernels: none -> 199 us  [the longest x3 55.2 us: multiply(): pl.pallas_call(kernel, in_specs=[scalars] * 3 + [anywhere] * many + [loca...]
    dot_general x7 -> x0, matrix products: 137 us -> none  [the longest x1 37 us: on_device(): jnp.einsum('mstik,mtkj->msij', stripes, one_rows, precision=highest)]
    gather x2 -> x12, local copies, waits for them, and re-layouts: 62.7 us -> 6.66 us  [the longest x6 3.33 us: on_device(): lists[:, m][:, second[span]]]
    mul x1 -> x0, other arithmetic: 28 us -> none  [on_device(): columns[clipped, node_index] * inside[:, :, None, None, None]]
  transfers between devices with their start and end apart: 10 -> 112, of which waited for: 8 -> 31; matrix products, arithmetic and copies ran while one was open for 6% -> 3% of each run, Pallas kernels for 0% -> 21%
where the time goes in v1:
time: 975 us; the launch traced here: 965 us
  waiting for transfers between devices  478 us (49%)
  starting transfers between devices  214 us (22%)
  Pallas kernels  199 us (20%)
  local copies, waits for them, and re-layouts  42 us (4%)
  between operations  18.1 us (2%)
    ppermute x93, waiting for transfers between devices, hop(): return lax.ppermute(value, 'col', pairs)  476 us
    ppermute x93, starting transfers between devices, hop(): return lax.ppermute(value, 'col', pairs)  211 us
    pallas_call x3, Pallas kernels, multiply(): pl.pallas_call(kernel, in_specs=[scalars] * 3 + [anywhere] * many + [loca...  55.2 us
    pallas_call x3, Pallas kernels, finish(): pl.pallas_call(kernel, in_specs=[scalars] * 2 + [anywhere] * many + [loca...  40.7 us
    pallas_call x6, Pallas kernels, select(): pl.pallas_call(kernel, grid_spec=pltpu.PrefetchScalarGridSpec(num_scalar_...  37.2 us
    pallas_call x3, Pallas kernels, change_base(): pl.pallas_call(kernel, in_specs=[scalars] + [anywhere] * many + [local, l...  25.3 us
  transfers between devices with their start and end apart: 112, of which 31 were waited for; matrix products, arithmetic and copies ran while one was open for 3% of the time, Pallas kernels for 21%

profile of v1, /device:TPU:0, one launch (start us, length us, event | category | flops | bytes accessed | tf_op | source)
XLA Modules:
  0.0 964.7 jit_solution(1930966017943879535)
XLA Ops:
  10.2 9.6 all-gather.2
  22.5 4.7 select_blocks.10
  30.0 4.9 select_blocks.8
  37.7 4.6 select_blocks.6
  45.5 7.5 select_blocks.11
  55.6 7.7 select_blocks.9
  67.3 4.4 collective-permute-start.52
  73.0 3.9 slice_bitcast_fusion.4
  76.8 5.5 collective-permute-start.60
  89.0 5.3 collective-permute-start.65
  95.6 7.7 select_blocks.7
  107.3 4.9 collective-permute-start.71
  112.9 9.8 %collective-permute-done.65.refs_7_.refs_9_ = f32[6,256,128]{2,1,0:T(8,128)} collective-permute-done((f32[6,256,128]{2,1,0:T(8,128)}, f32[6,256,128]{2,1,0:T(8,128)}, u32[]{:S(2)}, u32[]{:S(2)}) %collective-permute-start.65) | collective-permute-done | bytes 786464 | tf_op jit(solution)/shard_map/ppermute | solution.py:398
  123.4 16.0 %collective-permute-done.32.refs_2_ = f32[6,256,128]{2,1,0:T(8,128)S(1)} collective-permute-done((f32[6,256,128]{2,1,0:T(8,128)S(1)}, f32[6,256,128]{2,1,0:T(8,128)S(1)}, u32[]{:S(2)}, u32[]{:S(2)}) %collective-permute-start.32) | collective-permute-done | bytes 786464 | tf_op jit(solution)/shard_map/ppermute | solution.py:398
  139.4 4.4 collective-permute-start.76
  145.3 11.0 %collective-permute-done.71.refs_2_.refs_4_ = f32[6,256,128]{2,1,0:T(8,128)S(1)} collective-permute-done((f32[6,256,128]{2,1,0:T(8,128)S(1)}, f32[6,256,128]{2,1,0:T(8,128)S(1)}, u32[]{:S(2)}, u32[]{:S(2)}) %collective-permute-start.71) | collective-permute-done | bytes 786464 | tf_op jit(solution)/shard_map/ppermute | solution.py:398
  157.6 5.9 collective-permute-start.82
  164.2 8.9 collective-permute-done.76.refs_7_.refs_9_
  173.8 16.1 %collective-permute-done.12.refs_2_ = f32[6,256,128]{2,1,0:T(8,128)S(1)} collective-permute-done((f32[6,256,128]{2,1,0:T(8,128)S(1)}, f32[6,256,128]{2,1,0:T(8,128)S(1)}, u32[]{:S(2)}, u32[]{:S(2)}) %collective-permute-start.12) | collective-permute-done | bytes 786464 | tf_op jit(solution)/shard_map/ppermute | solution.py:398
  190.0 4.4 collective-permute-start.87
  196.0 10.8 %collective-permute-done.82.refs_2_.refs_4_ = f32[6,256,128]{2,1,0:T(8,128)} collective-permute-done((f32[6,256,128]{2,1,0:T(8,128)S(1)}, f32[6,256,128]{2,1,0:T(8,128)}, u32[]{:S(2)}, u32[]{:S(2)}) %collective-permute-start.82) | collective-permute-done | bytes 786464 | tf_op jit(solution)/shard_map/ppermute | solution.py:398
  209.6 10.8 %collective-permute-done.87.refs_7_.refs_9_ = f32[6,256,128]{2,1,0:T(8,128)S(1)} collective-permute-done((f32[6,256,128]{2,1,0:T(8,128)S(1)}, f32[6,256,128]{2,1,0:T(8,128)S(1)}, u32[]{:S(2)}, u32[]{:S(2)}) %collective-permute-start.87) | collective-permute-done | bytes 786464 | tf_op jit(solution)/shard_map/ppermute | solution.py:398
  227.9 22.1 %collective-permute-done.36.refs_5_ = f32[6,256,128]{2,1,0:T(8,128)} collective-permute-done((f32[6,256,128]{2,1,0:T(8,128)S(1)}, f32[6,256,128]{2,1,0:T(8,128)}, u32[]{:S(2)}, u32[]{:S(2)}) %collective-permute-start.36) | collective-permute-done | bytes 786464 | tf_op jit(solution)/shard_map/ppermute | solution.py:398
  257.4 38.8 %collective-permute-done.16.refs_5_ = f32[6,256,128]{2,1,0:T(8,128)S(1)} collective-permute-done((f32[6,256,128]{2,1,0:T(8,128)S(1)}, f32[6,256,128]{2,1,0:T(8,128)S(1)}, u32[]{:S(2)}, u32[]{:S(2)}) %collective-permute-start.16) | collective-permute-done | bytes 786464 | tf_op jit(solution)/shard_map/ppermute | solution.py:398
  301.6 27.7 %collective-permute-done.57.refs_6_ = f32[6,256,128]{2,1,0:T(8,128)} collective-permute-done((f32[6,256,128]{2,1,0:T(8,128)}, f32[6,256,128]{2,1,0:T(8,128)}, u32[]{:S(2)}, u32[]{:S(2)}) %collective-permute-start.57) | collective-permute-done | bytes 786464 | tf_op jit(solution)/shard_map/ppermute | solution.py:398
  332.3 4.6 fusion
  337.0 2.6 slice_bitcast_fusion.9
  339.6 8.5 change_base.5
  348.9 8.4 change_base.4
  358.8 3.2 collective-permute-done.17.refs_6_
  362.1 8.4 change_base.3
  374.7 38.3 %collective-permute-done.69.refs_11_.refs_13_ = f32[6,256,128]{2,1,0:T(8,128)} collective-permute-done((f32[6,256,128]{2,1,0:T(8,128)}, f32[6,256,128]{2,1,0:T(8,128)}, u32[]{:S(2)}, u32[]{:S(2)}) %collective-permute-start.69) | collective-permute-done | bytes 786464 | tf_op jit(solution)/shard_map/ppermute | solution.py:398
  415.8 4.6 collective-permute-start.20
  421.8 16.8 %collective-permute-start = (f32[5,256,128]{2,1,0:T(8,128)}, f32[5,256,128]{2,1,0:T(8,128)S(1)}, u32[]{:S(2)}, u32[]{:S(2)}) collective-permute-start(f32[5,256,128]{2,1,0:T(8,128)} %bitcast.162), channel_id=1, source_target_pairs={{0,1},{1,2},{2,3},{4,5},{5,6},{6,7},{8,9},{9,10},{10,11},{12,13},{... | collective-permute-start | bytes 1966088 | tf_op jit(solution)/shard_map/ppermute | solution.py:398
  445.2 7.2 collective-permute-done.23.refs_4_
  457.4 8.9 collective-permute-done.3.refs_4_
  467.9 14.1 %collective-permute-start.46 = (f32[10,256,128]{2,1,0:T(8,128)}, f32[10,256,128]{2,1,0:T(8,128)}, u32[]{:S(2)}, u32[]{:S(2)}) collective-permute-start(f32[10,256,128]{2,1,0:T(8,128)} %bitcast.149), channel_id=1, source_target_pairs={{0,1},{1,2},{2,3},{4,5},{5,6},{6,7},{8,9},{9,10},{10,11},{12,13},{... | collective-permute-start | bytes 3932168 | tf_op jit(solution)/shard_map/ppermute | solution.py:398
  483.3 11.8 %collective-permute-start.26 = (f32[10,256,128]{2,1,0:T(8,128)}, f32[10,256,128]{2,1,0:T(8,128)S(1)}, u32[]{:S(2)}, u32[]{:S(2)}) collective-permute-start(f32[10,256,128]{2,1,0:T(8,128)} %bitcast.146), channel_id=1, source_target_pairs={{0,1},{1,2},{2,3},{4,5},{5,6},{6,7},{8,9},{9,10},{10,11},{12,13},{... | collective-permute-start | bytes 3932168 | tf_op jit(solution)/shard_map/ppermute | solution.py:398
  497.9 35.2 %collective-permute-done.4.refs_5_ = f32[5,256,128]{2,1,0:T(8,128)S(1)} collective-permute-done((f32[5,256,128]{2,1,0:T(8,128)S(1)}, f32[5,256,128]{2,1,0:T(8,128)S(1)}, u32[]{:S(2)}, u32[]{:S(2)}) %collective-permute-start.4) | collective-permute-done | bytes 655392 | tf_op jit(solution)/shard_map/ppermute | solution.py:398
  536.5 13.7 %collective-permute-start.6 = (f32[10,256,128]{2,1,0:T(8,128)}, f32[10,256,128]{2,1,0:T(8,128)S(1)}, u32[]{:S(2)}, u32[]{:S(2)}) collective-permute-start(f32[10,256,128]{2,1,0:T(8,128)} %bitcast.153), channel_id=1, source_target_pairs={{0,1},{1,2},{2,3},{4,5},{5,6},{6,7},{8,9},{9,10},{10,11},{12,13},{... | collective-permute-start | bytes 3932168 | tf_op jit(solution)/shard_map/ppermute | solution.py:398
  552.3 23.8 %collective-permute-done.29.refs_4_ = f32[10,256,128]{2,1,0:T(8,128)} collective-permute-done((f32[10,256,128]{2,1,0:T(8,128)}, f32[10,256,128]{2,1,0:T(8,128)}, u32[]{:S(2)}, u32[]{:S(2)}) %collective-permute-start.29) | collective-permute-done | bytes 1310752 | tf_op jit(solution)/shard_map/ppermute | solution.py:398
  577.9 26.2 %collective-permute-done.9.refs_4_ = f32[10,256,128]{2,1,0:T(8,128)S(1)} collective-permute-done((f32[10,256,128]{2,1,0:T(8,128)}, f32[10,256,128]{2,1,0:T(8,128)S(1)}, u32[]{:S(2)}, u32[]{:S(2)}) %collective-permute-start.9) | collective-permute-done | bytes 1310752 | tf_op jit(solution)/shard_map/ppermute | solution.py:398
  608.5 23.7 %collective-permute-done.50.refs_5_ = f32[10,256,128]{2,1,0:T(8,128)S(1)} collective-permute-done((f32[10,256,128]{2,1,0:T(8,128)}, f32[10,256,128]{2,1,0:T(8,128)S(1)}, u32[]{:S(2)}, u32[]{:S(2)}) %collective-permute-start.50) | collective-permute-done | bytes 1310752 | tf_op jit(solution)/shard_map/ppermute | solution.py:398
  634.2 26.1 %collective-permute-done.30.refs_5_ = f32[10,256,128]{2,1,0:T(8,128)} collective-permute-done((f32[10,256,128]{2,1,0:T(8,128)}, f32[10,256,128]{2,1,0:T(8,128)}, u32[]{:S(2)}, u32[]{:S(2)}) %collective-permute-start.30) | collective-permute-done | bytes 1310752 | tf_op jit(solution)/shard_map/ppermute | solution.py:398
  662.1 26.4 %collective-permute-done.10.refs_5_ = f32[10,256,128]{2,1,0:T(8,128)} collective-permute-done((f32[10,256,128]{2,1,0:T(8,128)S(1)}, f32[10,256,128]{2,1,0:T(8,128)}, u32[]{:S(2)}, u32[]{:S(2)}) %collective-permute-start.10) | collective-permute-done | bytes 1310752 | tf_op jit(solution)/shard_map/ppermute | solution.py:398
  692.9 23.6 %collective-permute-done.51.refs_6_ = f32[10,256,128]{2,1,0:T(8,128)S(1)} collective-permute-done((f32[10,256,128]{2,1,0:T(8,128)S(1)}, f32[10,256,128]{2,1,0:T(8,128)S(1)}, u32[]{:S(2)}, u32[]{:S(2)}) %collective-permute-start.51) | collective-permute-done | bytes 1310752 | tf_op jit(solution)/shard_map/ppermute | solution.py:398
  718.8 18.4 %multiply.17 = (f32[5,256,384]{2,1,0:T(8,128)}, bf16[5,512,384]{2,1,0:T(8,128)(2,1)}, bf16[5,512,384]{2,1,0:T(8,128)(2,1)}, f32[4,256,384]{2,1,0:T(8,128)}, f32[4,256,384]{2,1,0:T(8,128)}) custom-call(s32[1]{0:T(128)} %bitcast.where, s32[1]{0:T(128)} %bitcast.1.row_at, s32[2,15]{1,0:T(2,128)} %constant.52.pair, f32[10,256,128]{2,1,0:T(8,128)} %copy-done.37, ...), custom_call_target="tpu_custom_call" | custom-call | tf_op jit(solution)/shard_map/multiply/pallas_call | solution.py:176
  737.4 7.3 collective-permute-done.31.refs_6_
  745.3 27.4 %collective-permute-done.11.refs_6_ = f32[10,256,128]{2,1,0:T(8,128)} collective-permute-done((f32[10,256,128]{2,1,0:T(8,128)}, f32[10,256,128]{2,1,0:T(8,128)}, u32[]{:S(2)}, u32[]{:S(2)}) %collective-permute-start.11) | collective-permute-done | bytes 1310752 | tf_op jit(solution)/shard_map/ppermute | solution.py:398
  774.0 18.3 %multiply.16 = (f32[5,256,384]{2,1,0:T(8,128)}, bf16[5,512,384]{2,1,0:T(8,128)(2,1)}, bf16[5,512,384]{2,1,0:T(8,128)(2,1)}, f32[4,256,384]{2,1,0:T(8,128)}, f32[4,256,384]{2,1,0:T(8,128)}) custom-call(s32[1]{0:T(128)} %bitcast.where, s32[1]{0:T(128)} %bitcast.1.row_at, s32[2,15]{1,0:T(2,128)} %constant.52.pair, ...), custom_call_target="tpu_custom_call" | custom-call | tf_op jit(solution)/shard_map/multiply/pallas_call | solution.py:176
  792.5 18.4 %multiply.15 = (f32[5,256,384]{2,1,0:T(8,128)}, bf16[5,512,384]{2,1,0:T(8,128)(2,1)}, bf16[5,512,384]{2,1,0:T(8,128)(2,1)}, f32[4,256,384]{2,1,0:T(8,128)}, f32[4,256,384]{2,1,0:T(8,128)}) custom-call(s32[1]{0:T(128)} %bitcast.where, s32[1]{0:T(128)} %bitcast.1.row_at, s32[2,15]{1,0:T(2,128)} %constant.52.pair, ...), custom_call_target="tpu_custom_call" | custom-call | tf_op jit(solution)/shard_map/multiply/pallas_call | solution.py:176
  814.7 16.9 %collective-permute-done.5.refs_6_ = f32[5,256,128]{2,1,0:T(8,128)S(1)} collective-permute-done((f32[5,256,128]{2,1,0:T(8,128)S(1)}, f32[5,256,128]{2,1,0:T(8,128)S(1)}, u32[]{:S(2)}, u32[]{:S(2)}) %collective-permute-start.5) | collective-permute-done | bytes 655392 | tf_op jit(solution)/shard_map/ppermute | solution.py:398
  833.8 13.6 %finish.3 = (f32[5,256,384]{2,1,0:T(8,128)}, f32[3,5,256,128]{3,2,1,0:T(8,128)}, f32[256,384]{1,0:T(8,128)}, f32[256,384]{1,0:T(8,128)}) custom-call(s32[1]{0:T(128)} %bitcast.where, s32[1]{0:T(128)} %bitcast.1.row_at, f32[5,256,128]{2,1,0:T(8,128)} %collective-permute-done.42.refs_0_, f32[5,256,128]{2,1,0:T(8,128)} %collective-permute-done.41.refs_1_, ...), custom_call_target="tpu_custom_call" | custom-call | tf_op jit(solution)/shard_map/finish/pallas_call | solution.py:233
  847.5 13.6 %finish.4 = (f32[5,256,384]{2,1,0:T(8,128)}, f32[3,5,256,128]{3,2,1,0:T(8,128)}, f32[256,384]{1,0:T(8,128)}, f32[256,384]{1,0:T(8,128)}) custom-call(s32[1]{0:T(128)} %bitcast.where, s32[1]{0:T(128)} %bitcast.1.row_at, f32[5,256,128]{2,1,0:T(8,128)} %copy-done.53, f32[5,256,128]{2,1,0:T(8,128)} %collective-permute-done.21.refs_1_, ...), custom_call_target="tpu_custom_call", output_to_operand_aliasing={{1}: (15, {})} | custom-call | tf_op jit(solution)/shard_map/finish/pallas_call | solution.py:233
  861.6 13.5 %finish.5 = (f32[5,256,384]{2,1,0:T(8,128)}, f32[3,5,256,128]{3,2,1,0:T(8,128)}, f32[256,384]{1,0:T(8,128)}, f32[256,384]{1,0:T(8,128)}) custom-call(s32[1]{0:T(128)} %bitcast.where, s32[1]{0:T(128)} %bitcast.1.row_at, f32[5,256,128]{2,1,0:T(8,128)} %copy-done.55, f32[5,256,128]{2,1,0:T(8,128)} %collective-permute-done.1.refs_1_, ...), custom_call_target="tpu_custom_call", output_to_operand_aliasing={{1}: (15, {})} | custom-call | tf_op jit(solution)/shard_map/finish/pallas_call | solution.py:233
  875.3 6.4 symmetric_upper.3.upper_ref
  881.7 6.6 symmetric_upper.4.upper_ref
  889.4 6.4 symmetric_upper.5.upper_ref
  896.6 4.9 symmetric_last.3
  901.6 4.9 symmetric_last.4
  910.1 6.3 collective-permute-start.99
  917.2 4.9 symmetric_last.5
  926.0 6.5 collective-permute-start.103
  935.2 8.7 collective-permute-start.95
  (422 shorter events, 150.0 us)
Async XLA Ops:
  8.0 329.0 %all-gather.5.cloned.1.call-start = ((), (), s32[]{:S(2)}) async-start(), calls=%async_computation.6 | async-start | bytes 2359296 | tf_op jit(solution)/shard_map/all_gather | solution.py:461
  10.1 402.8 %reduce-scatter.27.cloned.1.call-start = ((), (), s32[]{:S(2)}) async-start(), calls=%async_computation.11 | async-start | bytes 3276800
  27.3 388.5 %reduce-scatter.23.cloned.1.call-start = ((), (), s32[]{:S(2)}) async-start(), calls=%async_computation.9 | async-start | bytes 3276800
  35.0 386.8 %reduce-scatter.19.cloned.1.call-start = ((), (), s32[]{:S(2)}) async-start(), calls=%async_computation.7 | async-start | bytes 3276800
  42.3 425.5 %reduce-scatter.29.cloned.1.call-start = ((), (), s32[]{:S(2)}) async-start(), calls=%async_computation.12 | async-start | bytes 6553600
  53.0 430.2 %reduce-scatter.25.cloned.1.call-start = ((), (), s32[]{:S(2)}) async-start(), calls=%async_computation.10 | async-start | bytes 6553600
  63.4 471.8 %reduce-scatter.21.cloned.1.call-start = ((), (), s32[]{:S(2)}) async-start(), calls=%async_computation.8 | async-start | bytes 6553600
  104.6 34.8 %collective-permute-start.32 = (f32[6,256,128]{2,1,0:T(8,128)S(1)}, f32[6,256,128]{2,1,0:T(8,128)S(1)}, u32[]{:S(2)}, u32[]{:S(2)}) collective-permute-start(f32[6,256,128]{2,1,0:T(8,128)S(1)} %pad_maximum_fusion.1.refs_3_), channel_id=1, source_target_pairs={{0,1},{1,2},{2,3},{4,5},{5,6},{6,7},{8,9},{9,10},{10,11},{12,13},{... | collective-permute-start | bytes 2359304 | tf_op jit(solution)/shard_map/ppermute | solution.py:398
  106.0 38.0 %collective-permute-start.35 = (f32[6,256,128]{2,1,0:T(8,128)S(1)}, f32[6,256,128]{2,1,0:T(8,128)S(1)}, u32[]{:S(2)}, u32[]{:S(2)}) collective-permute-start(f32[6,256,128]{2,1,0:T(8,128)S(1)} %pad_maximum_fusion.1.refs_3_), channel_id=1, source_target_pairs={{1,0},{2,1},{3,2},{5,4},{6,5},{7,6},{9,8},{10,9},{11,10},{13,12},{... | collective-permute-start | bytes 2359304 | tf_op jit(solution)/shard_map/ppermute | solution.py:398
  107.3 49.0 %collective-permute-start.71 = (f32[6,256,128]{2,1,0:T(8,128)S(1)}, f32[6,256,128]{2,1,0:T(8,128)S(1)}, u32[]{:S(2)}, u32[]{:S(2)}) collective-permute-start(f32[6,256,128]{2,1,0:T(8,128)S(1)} %get-tuple-element.116.refs_3_.refs_5_), channel_id=1, source_target_pairs={{0,1},{1,2},{4,5},{5,6},{8,9},{9,10},{12,13},{13,14},{16,17},{17,1... | collective-permute-start | bytes 2359304 | tf_op jit(solution)/shard_map/ppermute | solution.py:398
  112.2 45.4 %collective-permute-start.78 = (f32[6,256,128]{2,1,0:T(8,128)S(1)}, f32[6,256,128]{2,1,0:T(8,128)S(1)}, u32[]{:S(2)}, u32[]{:S(2)}) collective-permute-start(f32[6,256,128]{2,1,0:T(8,128)S(1)} %get-tuple-element.115.refs_8_.refs_10_), channel_id=1, source_target_pairs={{2,1},{3,2},{6,5},{7,6},{10,9},{11,10},{14,13},{15,14},{18,17},{19... | collective-permute-start | bytes 2359304 | tf_op jit(solution)/shard_map/ppermute | solution.py:398
  122.7 40.9 %collective-permute-start.74 = (f32[6,256,128]{2,1,0:T(8,128)S(1)}, f32[6,256,128]{2,1,0:T(8,128)S(1)}, u32[]{:S(2)}, u32[]{:S(2)}) collective-permute-start(f32[6,256,128]{2,1,0:T(8,128)S(1)} %get-tuple-element.116.refs_3_.refs_5_), channel_id=1, source_target_pairs={{3,2},{7,6},{11,10},{15,14},{19,18},{23,22},{27,26},{31,30}} | collective-permute-start | bytes 2359304 | tf_op jit(solution)/shard_map/ppermute | solution.py:398
  144.0 46.0 %collective-permute-start.12 = (f32[6,256,128]{2,1,0:T(8,128)S(1)}, f32[6,256,128]{2,1,0:T(8,128)S(1)}, u32[]{:S(2)}, u32[]{:S(2)}) collective-permute-start(f32[6,256,128]{2,1,0:T(8,128)S(1)} %pad_maximum_fusion.refs_3_), channel_id=1, source_target_pairs={{0,1},{1,2},{2,3},{4,5},{5,6},{6,7},{8,9},{9,10},{10,11},{12,13},{... | collective-permute-start | bytes 2359304 | tf_op jit(solution)/shard_map/ppermute | solution.py:398
  156.3 38.1 %collective-permute-start.15 = (f32[6,256,128]{2,1,0:T(8,128)S(1)}, f32[6,256,128]{2,1,0:T(8,128)S(1)}, u32[]{:S(2)}, u32[]{:S(2)}) collective-permute-start(f32[6,256,128]{2,1,0:T(8,128)S(1)} %pad_maximum_fusion.refs_3_), channel_id=1, source_target_pairs={{1,0},{2,1},{3,2},{5,4},{6,5},{7,6},{9,8},{10,9},{11,10},{13,12},{... | collective-permute-start | bytes 2359304 | tf_op jit(solution)/shard_map/ppermute | solution.py:398
  157.6 49.2 %collective-permute-start.82 = (f32[6,256,128]{2,1,0:T(8,128)S(1)}, f32[6,256,128]{2,1,0:T(8,128)}, u32[]{:S(2)}, u32[]{:S(2)}) collective-permute-start(f32[6,256,128]{2,1,0:T(8,128)S(1)} %get-tuple-element.114.refs_3_.refs_5_), channel_id=1, source_target_pairs={{0,1},{1,2},{4,5},{5,6},{8,9},{9,10},{12,13},{13,14},{16,17},{17,1... | collective-permute-start | bytes 2359304 | tf_op jit(solution)/shard_map/ppermute | solution.py:398
  163.5 44.6 %collective-permute-start.89 = (f32[6,256,128]{2,1,0:T(8,128)S(1)}, f32[6,256,128]{2,1,0:T(8,128)S(1)}, u32[]{:S(2)}, u32[]{:S(2)}) collective-permute-start(f32[6,256,128]{2,1,0:T(8,128)S(1)} %get-tuple-element.113.refs_8_.refs_10_), channel_id=1, source_target_pairs={{2,1},{3,2},{6,5},{7,6},{10,9},{11,10},{14,13},{15,14},{18,17},{19... | collective-permute-start | bytes 2359304 | tf_op jit(solution)/shard_map/ppermute | solution.py:398
  173.1 35.7 %collective-permute-start.85 = (f32[6,256,128]{2,1,0:T(8,128)S(1)}, f32[6,256,128]{2,1,0:T(8,128)S(1)}, u32[]{:S(2)}, u32[]{:S(2)}) collective-permute-start(f32[6,256,128]{2,1,0:T(8,128)S(1)} %get-tuple-element.114.refs_3_.refs_5_), channel_id=1, source_target_pairs={{3,2},{7,6},{11,10},{15,14},{19,18},{23,22},{27,26},{31,30}} | collective-permute-start | bytes 2359304 | tf_op jit(solution)/shard_map/ppermute | solution.py:398
  250.8 45.5 %collective-permute-start.16 = (f32[6,256,128]{2,1,0:T(8,128)S(1)}, f32[6,256,128]{2,1,0:T(8,128)S(1)}, u32[]{:S(2)}, u32[]{:S(2)}) collective-permute-start(f32[6,256,128]{2,1,0:T(8,128)S(1)} %collective-permute-done.15.refs_4_), channel_id=1, source_target_pairs={{1,0},{2,1},{5,4},{6,5},{9,8},{10,9},{13,12},{14,13},{17,16},{18,1... | collective-permute-start | bytes 2359304 | tf_op jit(solution)/shard_map/ppermute | solution.py:398
  252.1 46.4 %collective-permute-start.83 = (f32[6,256,128]{2,1,0:T(8,128)}, f32[6,256,128]{2,1,0:T(8,128)S(1)}, u32[]{:S(2)}, u32[]{:S(2)}) collective-permute-start(f32[6,256,128]{2,1,0:T(8,128)} %collective-permute-done.82.refs_2_.refs_4_), channel_id=1, source_target_pairs={{1,2},{5,6},{9,10},{13,14},{17,18},{21,22},{25,26},{29,30}} | collective-permute-start | bytes 2359304 | tf_op jit(solution)/shard_map/ppermute | solution.py:398
  252.8 47.2 %collective-permute-start.54 = (f32[6,256,128]{2,1,0:T(8,128)}, f32[6,256,128]{2,1,0:T(8,128)}, u32[]{:S(2)}, u32[]{:S(2)}) collective-permute-start(f32[6,256,128]{2,1,0:T(8,128)} %collective-permute-done.53.refs_1_), channel_id=1, source_target_pairs={{2,3},{6,7},{10,11},{14,15},{18,19},{22,23},{26,27},{30,31}} | collective-permute-start | bytes 2359304 | tf_op jit(solution)/shard_map/ppermute | solution.py:398
  254.5 74.8 %collective-permute-start.57 = (f32[6,256,128]{2,1,0:T(8,128)}, f32[6,256,128]{2,1,0:T(8,128)}, u32[]{:S(2)}, u32[]{:S(2)}) collective-permute-start(f32[6,256,128]{2,1,0:T(8,128)} %collective-permute-done.56.refs_5_), channel_id=1, source_target_pairs={{1,0},{5,4},{9,8},{13,12},{17,16},{21,20},{25,24},{29,28}} | collective-permute-start | bytes 2359304 | tf_op jit(solution)/shard_map/ppermute | solution.py:398
  255.8 75.0 %collective-permute-start.34 = (f32[6,256,128]{2,1,0:T(8,128)S(1)}, f32[6,256,128]{2,1,0:T(8,128)}, u32[]{:S(2)}, u32[]{:S(2)}) collective-permute-start(f32[6,256,128]{2,1,0:T(8,128)S(1)} %collective-permute-done.33.refs_1_), channel_id=1, source_target_pairs={{2,3},{6,7},{10,11},{14,15},{18,19},{22,23},{26,27},{30,31}} | collective-permute-start | bytes 2359304 | tf_op jit(solution)/shard_map/ppermute | solution.py:398
  297.2 51.7 %collective-permute-start.37 = (f32[6,256,128]{2,1,0:T(8,128)}, f32[6,256,128]{2,1,0:T(8,128)}, u32[]{:S(2)}, u32[]{:S(2)}) collective-permute-start(f32[6,256,128]{2,1,0:T(8,128)} %collective-permute-done.36.refs_5_), channel_id=1, source_target_pairs={{1,0},{5,4},{9,8},{13,12},{17,16},{21,20},{25,24},{29,28}} | collective-permute-start | bytes 2359304 | tf_op jit(solution)/shard_map/ppermute | solution.py:398
  298.5 72.0 %collective-permute-start.90 = (f32[6,256,128]{2,1,0:T(8,128)S(1)}, f32[6,256,128]{2,1,0:T(8,128)}, u32[]{:S(2)}, u32[]{:S(2)}) collective-permute-start(f32[6,256,128]{2,1,0:T(8,128)S(1)} %collective-permute-done.89.refs_9_.refs_11_), channel_id=1, source_target_pairs={{2,1},{6,5},{10,9},{14,13},{18,17},{22,21},{26,25},{30,29}} | collective-permute-start | bytes 2359304 | tf_op jit(solution)/shard_map/ppermute | solution.py:398
  300.1 71.0 %collective-permute-start.86 = (f32[6,256,128]{2,1,0:T(8,128)S(1)}, f32[6,256,128]{2,1,0:T(8,128)}, u32[]{:S(2)}, u32[]{:S(2)}) collective-permute-start(f32[6,256,128]{2,1,0:T(8,128)S(1)} %collective-permute-done.85.refs_4_.refs_6_), channel_id=1, source_target_pairs={{2,1},{6,5},{10,9},{14,13},{18,17},{22,21},{26,25},{30,29}} | collective-permute-start | bytes 2359304 | tf_op jit(solution)/shard_map/ppermute | solution.py:398
  348.9 66.9 %collective-permute-start.58 = (f32[5,256,384]{2,1,0:T(8,128)}, f32[5,256,384]{2,1,0:T(8,128)}, u32[]{:S(2)}, u32[]{:S(2)}) collective-permute-start(f32[5,256,384]{2,1,0:T(8,128)} %get-tuple-element.72.refs_7_), channel_id=1, source_target_pairs={{0,4},{4,0},{1,5},{5,1},{2,6},{6,2},{3,7},{7,3},{8,12},{12,8},{9,1... | collective-permute-start | bytes 5898248 | tf_op jit(solution)/shard_map/ppermute | solution.py:390
  362.1 58.4 %collective-permute-start.38 = (f32[5,256,384]{2,1,0:T(8,128)}, f32[5,256,384]{2,1,0:T(8,128)}, u32[]{:S(2)}, u32[]{:S(2)}) collective-permute-start(f32[5,256,384]{2,1,0:T(8,128)} %get-tuple-element.65.refs_7_), channel_id=1, source_target_pairs={{0,4},{4,0},{1,5},{5,1},{2,6},{6,2},{3,7},{7,3},{8,12},{12,8},{9,1... | collective-permute-start | bytes 5898248 | tf_op jit(solution)/shard_map/ppermute | solution.py:390
  370.5 51.2 %collective-permute-start.18 = (f32[5,256,384]{2,1,0:T(8,128)}, f32[5,256,384]{2,1,0:T(8,128)}, u32[]{:S(2)}, u32[]{:S(2)}) collective-permute-start(f32[5,256,384]{2,1,0:T(8,128)} %get-tuple-element.58.refs_7_), channel_id=1, source_target_pairs={{0,4},{4,0},{1,5},{5,1},{2,6},{6,2},{3,7},{7,3},{8,12},{12,8},{9,1... | collective-permute-start | bytes 5898248 | tf_op jit(solution)/shard_map/ppermute | solution.py:390
  371.8 41.2 %collective-permute-start.69 = (f32[6,256,128]{2,1,0:T(8,128)}, f32[6,256,128]{2,1,0:T(8,128)}, u32[]{:S(2)}, u32[]{:S(2)}) collective-permute-start(f32[6,256,128]{2,1,0:T(8,128)} %copy-done.16), channel_id=1, source_target_pairs={{1,0},{5,4},{9,8},{13,12},{17,16},{21,20},{25,24},{29,28}} | collective-permute-start | bytes 2359304 | tf_op jit(solution)/shard_map/ppermute | solution.py:398
  374.0 40.4 %collective-permute-start.73 = (f32[6,256,128]{2,1,0:T(8,128)}, f32[6,256,128]{2,1,0:T(8,128)S(1)}, u32[]{:S(2)}, u32[]{:S(2)}) collective-permute-start(f32[6,256,128]{2,1,0:T(8,128)} %copy-done.20), channel_id=1, source_target_pairs={{2,3},{6,7},{10,11},{14,15},{18,19},{22,23},{26,27},{30,31}} | collective-permute-start | bytes 2359304 | tf_op jit(solution)/shard_map/ppermute | solution.py:398
  443.9 38.0 %collective-permute-start.44 = (f32[5,256,128]{2,1,0:T(8,128)}, f32[5,256,128]{2,1,0:T(8,128)}, u32[]{:S(2)}, u32[]{:S(2)}) collective-permute-start(f32[5,256,128]{2,1,0:T(8,128)} %collective-permute-done.43.refs_4_), channel_id=1, source_target_pairs={{1,0},{2,1},{5,4},{6,5},{9,8},{10,9},{13,12},{14,13},{17,16},{18,1... | collective-permute-start | bytes 1966088 | tf_op jit(solution)/shard_map/ppermute | solution.py:398
  456.1 38.9 %collective-permute-start.24 = (f32[5,256,128]{2,1,0:T(8,128)}, f32[5,256,128]{2,1,0:T(8,128)}, u32[]{:S(2)}, u32[]{:S(2)}) collective-permute-start(f32[5,256,128]{2,1,0:T(8,128)} %collective-permute-done.23.refs_4_), channel_id=1, source_target_pairs={{1,0},{2,1},{5,4},{6,5},{9,8},{10,9},{13,12},{14,13},{17,16},{18,1... | collective-permute-start | bytes 1966088 | tf_op jit(solution)/shard_map/ppermute | solution.py:398
  467.9 68.6 %collective-permute-start.46 = (f32[10,256,128]{2,1,0:T(8,128)}, f32[10,256,128]{2,1,0:T(8,128)}, u32[]{:S(2)}, u32[]{:S(2)}) collective-permute-start(f32[10,256,128]{2,1,0:T(8,128)} %bitcast.149), channel_id=1, source_target_pairs={{0,1},{1,2},{2,3},{4,5},{5,6},{6,7},{8,9},{9,10},{10,11},{12,13},{... | collective-permute-start | bytes 3932168 | tf_op jit(solution)/shard_map/ppermute | solution.py:398
  481.9 68.3 %collective-permute-start.49 = (f32[10,256,128]{2,1,0:T(8,128)}, f32[10,256,128]{2,1,0:T(8,128)}, u32[]{:S(2)}, u32[]{:S(2)}) collective-permute-start(f32[10,256,128]{2,1,0:T(8,128)} %bitcast.150), channel_id=1, source_target_pairs={{1,0},{2,1},{3,2},{5,4},{6,5},{7,6},{9,8},{10,9},{11,10},{13,12},{... | collective-permute-start | bytes 3932168 | tf_op jit(solution)/shard_map/ppermute | solution.py:398
  483.3 67.7 %collective-permute-start.26 = (f32[10,256,128]{2,1,0:T(8,128)}, f32[10,256,128]{2,1,0:T(8,128)S(1)}, u32[]{:S(2)}, u32[]{:S(2)}) collective-permute-start(f32[10,256,128]{2,1,0:T(8,128)} %bitcast.146), channel_id=1, source_target_pairs={{0,1},{1,2},{2,3},{4,5},{5,6},{6,7},{8,9},{9,10},{10,11},{12,13},{... | collective-permute-start | bytes 3932168 | tf_op jit(solution)/shard_map/ppermute | solution.py:398
  495.1 38.0 %collective-permute-start.4 = (f32[5,256,128]{2,1,0:T(8,128)S(1)}, f32[5,256,128]{2,1,0:T(8,128)S(1)}, u32[]{:S(2)}, u32[]{:S(2)}) collective-permute-start(f32[5,256,128]{2,1,0:T(8,128)S(1)} %collective-permute-done.3.refs_4_), channel_id=1, source_target_pairs={{1,0},{2,1},{5,4},{6,5},{9,8},{10,9},{13,12},{14,13},{17,16},{18,1... | collective-permute-start | bytes 1966088 | tf_op jit(solution)/shard_map/ppermute | solution.py:398
  496.4 38.8 %collective-permute-start.42 = (f32[5,256,128]{2,1,0:T(8,128)}, f32[5,256,128]{2,1,0:T(8,128)}, u32[]{:S(2)}, u32[]{:S(2)}) collective-permute-start(f32[5,256,128]{2,1,0:T(8,128)} %collective-permute-done.41.refs_1_), channel_id=1, source_target_pairs={{2,3},{6,7},{10,11},{14,15},{18,19},{22,23},{26,27},{30,31}} | collective-permute-start | bytes 1966088 | tf_op jit(solution)/shard_map/ppermute | solution.py:398
  533.9 42.3 %collective-permute-start.29 = (f32[10,256,128]{2,1,0:T(8,128)}, f32[10,256,128]{2,1,0:T(8,128)}, u32[]{:S(2)}, u32[]{:S(2)}) collective-permute-start(f32[10,256,128]{2,1,0:T(8,128)} %bitcast.147), channel_id=1, source_target_pairs={{1,0},{2,1},{3,2},{5,4},{6,5},{7,6},{9,8},{10,9},{11,10},{13,12},{... | collective-permute-start | bytes 3932168 | tf_op jit(solution)/shard_map/ppermute | solution.py:398
  535.2 68.9 %collective-permute-start.9 = (f32[10,256,128]{2,1,0:T(8,128)}, f32[10,256,128]{2,1,0:T(8,128)S(1)}, u32[]{:S(2)}, u32[]{:S(2)}) collective-permute-start(f32[10,256,128]{2,1,0:T(8,128)} %bitcast.152), channel_id=1, source_target_pairs={{1,0},{2,1},{3,2},{5,4},{6,5},{7,6},{9,8},{10,9},{11,10},{13,12},{... | collective-permute-start | bytes 3932168 | tf_op jit(solution)/shard_map/ppermute | solution.py:398
  536.5 68.9 %collective-permute-start.6 = (f32[10,256,128]{2,1,0:T(8,128)}, f32[10,256,128]{2,1,0:T(8,128)S(1)}, u32[]{:S(2)}, u32[]{:S(2)}) collective-permute-start(f32[10,256,128]{2,1,0:T(8,128)} %bitcast.153), channel_id=1, source_target_pairs={{0,1},{1,2},{2,3},{4,5},{5,6},{6,7},{8,9},{9,10},{10,11},{12,13},{... | collective-permute-start | bytes 3932168 | tf_op jit(solution)/shard_map/ppermute | solution.py:398
  550.2 56.5 %collective-permute-start.47 = (f32[10,256,128]{2,1,0:T(8,128)}, f32[10,256,128]{2,1,0:T(8,128)S(1)}, u32[]{:S(2)}, u32[]{:S(2)}) collective-permute-start(f32[10,256,128]{2,1,0:T(8,128)} %collective-permute-done.46.refs_2_), channel_id=1, source_target_pairs={{1,2},{2,3},{5,6},{6,7},{9,10},{10,11},{13,14},{14,15},{17,18},{18... | collective-permute-start | bytes 3932168 | tf_op jit(solution)/shard_map/ppermute | solution.py:398
  551.0 81.2 %collective-permute-start.50 = (f32[10,256,128]{2,1,0:T(8,128)}, f32[10,256,128]{2,1,0:T(8,128)S(1)}, u32[]{:S(2)}, u32[]{:S(2)}) collective-permute-start(f32[10,256,128]{2,1,0:T(8,128)} %collective-permute-done.49.refs_4_), channel_id=1, source_target_pairs={{1,0},{2,1},{5,4},{6,5},{9,8},{10,9},{13,12},{14,13},{17,16},{18,1... | collective-permute-start | bytes 3932168 | tf_op jit(solution)/shard_map/ppermute | solution.py:398
  576.1 56.8 %collective-permute-start.27 = (f32[10,256,128]{2,1,0:T(8,128)S(1)}, f32[10,256,128]{2,1,0:T(8,128)}, u32[]{:S(2)}, u32[]{:S(2)}) collective-permute-start(f32[10,256,128]{2,1,0:T(8,128)S(1)} %collective-permute-done.26.refs_2_), channel_id=1, source_target_pairs={{1,2},{2,3},{5,6},{6,7},{9,10},{10,11},{13,14},{14,15},{17,18},{18... | collective-permute-start | bytes 3932168 | tf_op jit(solution)/shard_map/ppermute | solution.py:398
  604.1 56.3 %collective-permute-start.30 = (f32[10,256,128]{2,1,0:T(8,128)}, f32[10,256,128]{2,1,0:T(8,128)}, u32[]{:S(2)}, u32[]{:S(2)}) collective-permute-start(f32[10,256,128]{2,1,0:T(8,128)} %collective-permute-done.29.refs_4_), channel_id=1, source_target_pairs={{1,0},{2,1},{5,4},{6,5},{9,8},{10,9},{13,12},{14,13},{17,16},{18,1... | collective-permute-start | bytes 3932168 | tf_op jit(solution)/shard_map/ppermute | solution.py:398
  605.4 83.1 %collective-permute-start.10 = (f32[10,256,128]{2,1,0:T(8,128)S(1)}, f32[10,256,128]{2,1,0:T(8,128)}, u32[]{:S(2)}, u32[]{:S(2)}) collective-permute-start(f32[10,256,128]{2,1,0:T(8,128)S(1)} %collective-permute-done.9.refs_4_), channel_id=1, source_target_pairs={{1,0},{2,1},{5,4},{6,5},{9,8},{10,9},{13,12},{14,13},{17,16},{18,1... | collective-permute-start | bytes 3932168 | tf_op jit(solution)/shard_map/ppermute | solution.py:398
  606.7 83.0 %collective-permute-start.7 = (f32[10,256,128]{2,1,0:T(8,128)S(1)}, f32[10,256,128]{2,1,0:T(8,128)}, u32[]{:S(2)}, u32[]{:S(2)}) collective-permute-start(f32[10,256,128]{2,1,0:T(8,128)S(1)} %collective-permute-done.6.refs_2_), channel_id=1, source_target_pairs={{1,2},{2,3},{5,6},{6,7},{9,10},{10,11},{13,14},{14,15},{17,18},{18... | collective-permute-start | bytes 3932168 | tf_op jit(solution)/shard_map/ppermute | solution.py:398
  632.2 58.9 %collective-permute-start.48 = (f32[10,256,128]{2,1,0:T(8,128)S(1)}, f32[10,256,128]{2,1,0:T(8,128)S(1)}, u32[]{:S(2)}, u32[]{:S(2)}) collective-permute-start(f32[10,256,128]{2,1,0:T(8,128)S(1)} %collective-permute-done.47.refs_1_), channel_id=1, source_target_pairs={{2,3},{6,7},{10,11},{14,15},{18,19},{22,23},{26,27},{30,31}} | collective-permute-start | bytes 3932168 | tf_op jit(solution)/shard_map/ppermute | solution.py:398
  632.9 83.5 %collective-permute-start.51 = (f32[10,256,128]{2,1,0:T(8,128)S(1)}, f32[10,256,128]{2,1,0:T(8,128)S(1)}, u32[]{:S(2)}, u32[]{:S(2)}) collective-permute-start(f32[10,256,128]{2,1,0:T(8,128)S(1)} %collective-permute-done.50.refs_5_), channel_id=1, source_target_pairs={{1,0},{5,4},{9,8},{13,12},{17,16},{21,20},{25,24},{29,28}} | collective-permute-start | bytes 3932168 | tf_op jit(solution)/shard_map/ppermute | solution.py:398
  660.4 76.9 %collective-permute-start.28 = (f32[10,256,128]{2,1,0:T(8,128)}, f32[10,256,128]{2,1,0:T(8,128)}, u32[]{:S(2)}, u32[]{:S(2)}) collective-permute-start(f32[10,256,128]{2,1,0:T(8,128)} %collective-permute-done.27.refs_1_), channel_id=1, source_target_pairs={{2,3},{6,7},{10,11},{14,15},{18,19},{22,23},{26,27},{30,31}} | collective-permute-start | bytes 3932168 | tf_op jit(solution)/shard_map/ppermute | solution.py:398
  688.5 56.2 %collective-permute-start.31 = (f32[10,256,128]{2,1,0:T(8,128)}, f32[10,256,128]{2,1,0:T(8,128)}, u32[]{:S(2)}, u32[]{:S(2)}) collective-permute-start(f32[10,256,128]{2,1,0:T(8,128)} %collective-permute-done.30.refs_5_), channel_id=1, source_target_pairs={{1,0},{5,4},{9,8},{13,12},{17,16},{21,20},{25,24},{29,28}} | collective-permute-start | bytes 3932168 | tf_op jit(solution)/shard_map/ppermute | solution.py:398
  689.8 83.0 %collective-permute-start.11 = (f32[10,256,128]{2,1,0:T(8,128)}, f32[10,256,128]{2,1,0:T(8,128)}, u32[]{:S(2)}, u32[]{:S(2)}) collective-permute-start(f32[10,256,128]{2,1,0:T(8,128)} %collective-permute-done.10.refs_5_), channel_id=1, source_target_pairs={{1,0},{5,4},{9,8},{13,12},{17,16},{21,20},{25,24},{29,28}} | collective-permute-start | bytes 3932168 | tf_op jit(solution)/shard_map/ppermute | solution.py:398
  691.1 101.2 %collective-permute-start.8 = (f32[10,256,128]{2,1,0:T(8,128)}, f32[10,256,128]{2,1,0:T(8,128)}, u32[]{:S(2)}, u32[]{:S(2)}) collective-permute-start(f32[10,256,128]{2,1,0:T(8,128)} %collective-permute-done.7.refs_1_), channel_id=1, source_target_pairs={{2,3},{6,7},{10,11},{14,15},{18,19},{22,23},{26,27},{30,31}} | collective-permute-start | bytes 3932168 | tf_op jit(solution)/shard_map/ppermute | solution.py:398
  717.5 93.4 %collective-permute-start.45 = (f32[5,256,128]{2,1,0:T(8,128)}, f32[5,256,128]{2,1,0:T(8,128)}, u32[]{:S(2)}, u32[]{:S(2)}) collective-permute-start(f32[5,256,128]{2,1,0:T(8,128)} %collective-permute-done.44.refs_5_), channel_id=1, source_target_pairs={{1,0},{5,4},{9,8},{13,12},{17,16},{21,20},{25,24},{29,28}} | collective-permute-start | bytes 1966088 | tf_op jit(solution)/shard_map/ppermute | solution.py:398
  737.3 95.0 %collective-permute-start.59 = (f32[4,256,384]{2,1,0:T(8,128)}, f32[4,256,384]{2,1,0:T(8,128)}, u32[]{:S(2)}, u32[]{:S(2)}) collective-permute-start(f32[4,256,384]{2,1,0:T(8,128)} %get-tuple-element.78), channel_id=1, source_target_pairs={{0,4},{4,0},{1,5},{5,1},{2,6},{6,2},{3,7},{7,3},{8,12},{12,8},{9,1... | collective-permute-start | bytes 4718600 | tf_op jit(solution)/shard_map/ppermute | solution.py:390
  744.6 66.7 %collective-permute-start.22 = (f32[5,256,128]{2,1,0:T(8,128)}, f32[5,256,128]{2,1,0:T(8,128)S(1)}, u32[]{:S(2)}, u32[]{:S(2)}) collective-permute-start(f32[5,256,128]{2,1,0:T(8,128)} %collective-permute-done.21.refs_1_), channel_id=1, source_target_pairs={{2,3},{6,7},{10,11},{14,15},{18,19},{22,23},{26,27},{30,31}} | collective-permute-start | bytes 1966088 | tf_op jit(solution)/shard_map/ppermute | solution.py:398
  772.7 39.3 %collective-permute-start.25 = (f32[5,256,128]{2,1,0:T(8,128)}, f32[5,256,128]{2,1,0:T(8,128)S(1)}, u32[]{:S(2)}, u32[]{:S(2)}) collective-permute-start(f32[5,256,128]{2,1,0:T(8,128)} %collective-permute-done.24.refs_5_), channel_id=1, source_target_pairs={{1,0},{5,4},{9,8},{13,12},{17,16},{21,20},{25,24},{29,28}} | collective-permute-start | bytes 1966088 | tf_op jit(solution)/shard_map/ppermute | solution.py:398
  792.4 55.0 %collective-permute-start.39 = (f32[4,256,384]{2,1,0:T(8,128)}, f32[4,256,384]{2,1,0:T(8,128)}, u32[]{:S(2)}, u32[]{:S(2)}) collective-permute-start(f32[4,256,384]{2,1,0:T(8,128)} %get-tuple-element.71), channel_id=1, source_target_pairs={{0,4},{4,0},{1,5},{5,1},{2,6},{6,2},{3,7},{7,3},{8,12},{12,8},{9,1... | collective-permute-start | bytes 4718600 | tf_op jit(solution)/shard_map/ppermute | solution.py:390
  810.9 50.2 %collective-permute-start.19 = (f32[4,256,384]{2,1,0:T(8,128)}, f32[4,256,384]{2,1,0:T(8,128)}, u32[]{:S(2)}, u32[]{:S(2)}) collective-permute-start(f32[4,256,384]{2,1,0:T(8,128)} %get-tuple-element.64), channel_id=1, source_target_pairs={{0,4},{4,0},{1,5},{5,1},{2,6},{6,2},{3,7},{7,3},{8,12},{12,8},{9,1... | collective-permute-start | bytes 4718600 | tf_op jit(solution)/shard_map/ppermute | solution.py:390
  813.4 61.8 %collective-permute-start.80 = (f32[6,256,128]{2,1,0:T(8,128)S(1)}, f32[6,256,128]{2,1,0:T(8,128)}, u32[]{:S(2)}, u32[]{:S(2)}) collective-permute-start(f32[6,256,128]{2,1,0:T(8,128)S(1)} %copy-done.23), channel_id=1, source_target_pairs={{1,0},{5,4},{9,8},{13,12},{17,16},{21,20},{25,24},{29,28}} | collective-permute-start | bytes 2359304 | tf_op jit(solution)/shard_map/ppermute | solution.py:398
  831.6 56.7 %collective-permute-start.84 = (f32[6,256,128]{2,1,0:T(8,128)S(1)}, f32[6,256,128]{2,1,0:T(8,128)S(1)}, u32[]{:S(2)}, u32[]{:S(2)}) collective-permute-start(f32[6,256,128]{2,1,0:T(8,128)S(1)} %copy-done.18), channel_id=1, source_target_pairs={{2,3},{6,7},{10,11},{14,15},{18,19},{22,23},{26,27},{30,31}} | collective-permute-start | bytes 2359304 | tf_op jit(solution)/shard_map/ppermute | solution.py:398
  832.3 56.0 %collective-permute-start.91 = (f32[6,256,128]{2,1,0:T(8,128)}, f32[6,256,128]{2,1,0:T(8,128)S(1)}, u32[]{:S(2)}, u32[]{:S(2)}) collective-permute-start(f32[6,256,128]{2,1,0:T(8,128)} %collective-permute-done.90.refs_10_.refs_12_), channel_id=1, source_target_pairs={{1,0},{5,4},{9,8},{13,12},{17,16},{21,20},{25,24},{29,28}} | collective-permute-start | bytes 2359304 | tf_op jit(solution)/shard_map/ppermute | solution.py:398
  847.4 48.5 %collective-permute-start.70 = (f32[256,384]{1,0:T(8,128)}, f32[256,384]{1,0:T(8,128)S(1)}, u32[]{:S(2)}, u32[]{:S(2)}) collective-permute-start(f32[256,384]{1,0:T(8,128)} %get-tuple-element.85), channel_id=1, source_target_pairs={{0,4},{4,0},{1,5},{5,1},{2,6},{6,2},{3,7},{7,3},{8,12},{12,8},{9,1... | collective-permute-start | bytes 1179656 | tf_op jit(solution)/shard_map/ppermute | solution.py:390
  861.1 40.5 %collective-permute-start.81 = (f32[256,384]{1,0:T(8,128)}, f32[256,384]{1,0:T(8,128)}, u32[]{:S(2)}, u32[]{:S(2)}) collective-permute-start(f32[256,384]{1,0:T(8,128)} %get-tuple-element.90), channel_id=1, source_target_pairs={{0,4},{4,0},{1,5},{5,1},{2,6},{6,2},{3,7},{7,3},{8,12},{12,8},{9,1... | collective-permute-start | bytes 1179656 | tf_op jit(solution)/shard_map/ppermute | solution.py:390
  875.2 41.3 %collective-permute-start.92 = (f32[256,384]{1,0:T(8,128)}, f32[256,384]{1,0:T(8,128)S(1)}, u32[]{:S(2)}, u32[]{:S(2)}) collective-permute-start(f32[256,384]{1,0:T(8,128)} %get-tuple-element.96), channel_id=1, source_target_pairs={{0,4},{4,0},{1,5},{5,1},{2,6},{6,2},{3,7},{7,3},{8,12},{12,8},{9,1... | collective-permute-start | bytes 1179656 | tf_op jit(solution)/shard_map/ppermute | solution.py:390
  (125 other events, 4651.5 us)
Sparse Core Ops, SparseCore 0:
  10.4 12.5 all-gather.4
Sparse Core Ops, SparseCore 1:
  27.4 39.7 reduce-scatter.26
  70.0 39.4 reduce-scatter.22
  113.0 39.4 reduce-scatter.18
  155.5 61.2 reduce-scatter.28
  219.7 61.2 reduce-scatter.24
  284.0 61.2 reduce-scatter.20
